TPU v7x, 512 devices: a whole 4x4x16 slice. The times are simulated.
512 devices in a mesh: dp: 32 (over y, x, core), mp: 16 (over z).
Axes of the slice: x: 4, y: 4, z: 16, core: 2. Of those that a mesh axis runs over, the one named last changes fastest.
Arguments:
- tokens: bfloat16 [32768, 8192], P('dp', 'mp'), may hold values from -6 to 6
- value_weight: bfloat16 [8192, 1024], P('mp'), may hold values from -0.0625 to 0.0625
- down_panels: bfloat16 [256, 8192, 64], P('dp', 'mp'), may hold values from -0.0625 to 0.0625
- up_panels: bfloat16 [256, 64, 1024], P('dp'), may hold values from -0.75 to 0.75
- cotangent: bfloat16 [32768, 1024], P(('dp', 'mp')), may hold values from -6 to 6
- block_adapter: int32 [256], replicated, may hold values from 0 to 255, as said below
- adapter_slot: int32 [256], replicated, may hold values from 0 to 255, as said below
Outputs:
- projected: bfloat16 [32768, 1024], P(('dp', 'mp'))
- grad_tokens: bfloat16 [32768, 8192], P('dp', 'mp')
- grad_down: bfloat16 [256, 8192, 64], P('dp', 'mp')
- grad_up: bfloat16 [256, 64, 1024], P('dp')
Inputs may be any that keep to these rules, and one draw needn't show every extreme that they name: `block_adapter`: the 8 blocks of one index of dp name adapters stored on 8 different owners, the owner of slot s being s // 8. `adapter_slot`: A permutation of the adapters.
All inputs are finite; a program needn't handle non-finite values.
Results may differ from a plain program's by a relative error of at most 0.005.
Values may be sent and summed in bfloat16 or wider, within the bound.
A program may use at most 128 MiB of HBM per device.

v0:
```python
import jax
import jax.numpy as jnp
from jax import lax
from jax.sharding import PartitionSpec as P

RANK = 64
BLOCK_ROWS = 128


def per_device(
    tokens, value_weight, down_panels, up_panels, cotangent, block_adapter, adapter_slot
):
    n_owners = lax.axis_size("dp")
    myself = lax.axis_index("dp")
    n_split = lax.axis_size("mp")
    my_part = lax.axis_index("mp")
    rows, width_dev = tokens.shape
    own_rows, kv_full = cotangent.shape
    kv_part = kv_full // n_split
    stored = down_panels.shape[0]
    blocks = rows // BLOCK_ROWS
    highest = lax.Precision.HIGHEST
    hits = block_adapter[:, None] == jnp.arange(adapter_slot.shape[0], dtype=jnp.int32)[None, :]
    slots_all = jnp.sum(jnp.where(hits, adapter_slot[None, :], 0), axis=1)
    owner_all = (slots_all // stored).reshape(n_owners, blocks)
    local_all = (slots_all % stored).reshape(n_owners, blocks)
    mine = owner_all == myself
    wanted = jnp.sum(jnp.where(mine, local_all, 0), axis=1)
    served = jnp.any(mine, axis=1)
    pick_mask = (wanted[:, None] == jnp.arange(stored, dtype=jnp.int32)[None, :]) & served[:, None]
    my_owner = lax.dynamic_index_in_dim(owner_all, myself, 0, keepdims=False)
    select_mask = my_owner[:, None] == jnp.arange(n_owners, dtype=jnp.int32)[None, :]
    select_f32 = select_mask.astype(jnp.float32)
    send_a = jnp.take(down_panels, wanted, axis=0)
    up_cols = lax.dynamic_slice_in_dim(up_panels, my_part * kv_part, kv_part, 2)
    send_b = jnp.take(up_cols, wanted, axis=0)
    got_a = lax.all_to_all(send_a, "dp", split_axis=0, concat_axis=0, tiled=True)
    got_b = lax.all_to_all(send_b, "dp", split_axis=0, concat_axis=0, tiled=True)
    panel_a = jnp.take(got_a, my_owner, axis=0)
    panel_b_cols = jnp.take(got_b, my_owner, axis=0)
    first_row = my_part * own_rows
    part_block = jnp.arange(n_split, dtype=jnp.int32) * own_rows // BLOCK_ROWS
    to_parts = jnp.take(panel_b_cols, part_block, axis=0)
    from_parts = lax.all_to_all(to_parts, "mp", split_axis=0, concat_axis=0, tiled=True)
    my_up = from_parts.transpose(1, 0, 2).reshape(RANK, kv_full)
    token_blocks = tokens.reshape(blocks, BLOCK_ROWS, width_dev)
    partial_value = jnp.dot(tokens, value_weight, preferred_element_type=jnp.float32)
    base = lax.psum_scatter(partial_value, "mp", scatter_dimension=0, tiled=True)
    down_part = jnp.einsum(
        "bnd,bdk->bnk", token_blocks, panel_a, preferred_element_type=jnp.float32
    )
    down = lax.psum(down_part, "mp").astype(jnp.bfloat16)
    my_down = lax.dynamic_slice_in_dim(down.reshape(rows, RANK), first_row, own_rows, 0)
    lifted = jnp.dot(my_down, my_up, preferred_element_type=jnp.float32)
    projected = (base + lifted).astype(jnp.bfloat16)
    my_back = jnp.einsum("nc,kc->nk", cotangent, my_up, preferred_element_type=jnp.float32).astype(
        jnp.bfloat16
    )
    back = lax.all_gather(my_back, "mp", axis=0, tiled=True).reshape(blocks, BLOCK_ROWS, RANK)
    cot_all = lax.all_gather(cotangent, "mp", axis=0, tiled=True)
    grad_base = jnp.einsum("nc,dc->nd", cot_all, value_weight, preferred_element_type=jnp.float32)
    through = jnp.einsum("bnk,bdk->bnd", back, panel_a, preferred_element_type=jnp.float32)
    grad_tokens = (grad_base + through.reshape(rows, width_dev)).astype(jnp.bfloat16)
    block_grad_a = jnp.einsum(
        "bnd,bnk->bdk", token_blocks, back, preferred_element_type=jnp.float32
    ).astype(jnp.bfloat16)
    cot_blocks = cot_all.reshape(blocks, BLOCK_ROWS, kv_full)
    cot_share = lax.dynamic_slice_in_dim(cot_blocks, my_part * kv_part, kv_part, 2)
    block_grad_b = jnp.einsum(
        "bnk,bnc->bkc",
        down.reshape(blocks, BLOCK_ROWS, RANK),
        cot_share,
        preferred_element_type=jnp.float32,
    )
    send_ga = jnp.einsum(
        "bo,bdk->odk",
        select_mask.astype(jnp.bfloat16),
        block_grad_a,
        preferred_element_type=jnp.float32,
    ).astype(jnp.bfloat16)
    send_gb = jnp.einsum("bo,bkc->okc", select_f32, block_grad_b, precision=highest)
    recv_ga = lax.all_to_all(send_ga, "dp", split_axis=0, concat_axis=0, tiled=True)
    recv_gb = lax.all_to_all(send_gb, "dp", split_axis=0, concat_axis=0, tiled=True)
    pick_f32 = pick_mask.astype(jnp.float32)
    grad_down = jnp.einsum(
        "ra,rdk->adk", pick_mask.astype(jnp.bfloat16), recv_ga, preferred_element_type=jnp.float32
    ).astype(jnp.bfloat16)
    grad_share = jnp.einsum("ra,rkc->akc", pick_f32, recv_gb, precision=highest).astype(
        jnp.bfloat16
    )
    grad_up = lax.all_gather(grad_share, "mp", axis=2, tiled=True)
    return (projected, grad_tokens, grad_down, grad_up)


def solution(mesh):
    placed = (
        P("dp", "mp"),
        P("mp", None),
        P("dp", "mp", None),
        P("dp", None, None),
        P(("dp", "mp"), None),
        P(),
        P(),
    )
    return jax.shard_map(
        per_device,
        mesh=mesh,
        in_specs=placed,
        out_specs=(P(("dp", "mp"), None), P("dp", "mp"), P("dp", "mp", None), P("dp", None, None)),
        check_vma=False,
    )
```

profile of v0, /device:TPU:4, one launch (start us, length us, event | category | flops | bytes accessed | tf_op | source)
XLA Modules:
  0.0 297.7 jit_solution(200860388559841904)
XLA Ops:
  7.2 0.0 copy-start
  7.2 0.0 all-gather.3.cloned.1.call-start
  7.2 0.7 all-gather.3.cloned.1.call-update
  7.9 0.9 select_reduce_fusion
  8.8 0.1 reduce_sum.23
  8.9 0.1 fusion.43
  9.0 0.1 fusion.18
  9.2 1.7 gather_fusion
  10.9 1.6 broadcast_select_fusion
  12.5 10.2 %all-to-all-start = ((bf16[32,512,64]{1,2,0:T(8,128)(2,1)}), bf16[32,512,64]{1,2,0:T(8,128)(2,1)}, u32[]{:S(2)}, u32[]{:S(2)}) async-start(bf16[32,512,64]{1,2,0:T(8,128)(2,1)} %broadcast_select_fusion), calls=%async_computation.1 | async-start | bytes 4194304 | tf_op jit(solution)/shard_map/all_to_all | solution.py:37
  22.7 0.0 all-gather.5.cloned.1.call-start
  22.8 26.6 %all-to-all-done = bf16[32,512,64]{1,2,0:T(8,128)(2,1)} async-done(((bf16[32,512,64]{1,2,0:T(8,128)(2,1)}), bf16[32,512,64]{1,2,0:T(8,128)(2,1)}, u32[]{:S(2)}, u32[]{:S(2)}) %all-to-all-start) | async-done | bytes 2097184 | tf_op jit(solution)/shard_map/all_to_all | solution.py:37
  49.4 2.2 gather_fusion.1
  51.5 0.0 copy-start.1
  51.6 0.5 convolution_bitcast_fusion
  52.1 62.3 %all-reduce.1 = bf16[8,128,64]{1,2,0:T(8,128)(2,1)S(1)} all-reduce(f32[8,128,64]{1,2,0:T(8,128)S(1)} %convolution_bitcast_fusion), channel_id=1, replica_groups=mesh['dp'=32,'mp'=16] {'mp'}, use_global_device_ids=true, to_apply=%region_3.4 | all-reduce | flops 65536 | bytes 393216 | tf_op jit(solution)/shard_map/psum | solution.py:52
  114.4 0.0 copy-start.3
  114.4 0.0 all-gather.3.cloned.1.call-done
  114.5 1.2 fusion.13
  115.7 0.7 fusion.11
  116.4 0.6 copy.58
  117.1 0.7 reshape.206
  117.7 16.3 %all_to_all.25 = f32[32,1,4096]{2,1,0:T(1,128)S(1)} all-to-all(f32[32,1,4096]{2,1,0:T(1,128)S(1)} %reshape.206), channel_id=1, replica_groups=mesh['dp'=32,'mp'=16] {'dp'}, dimensions={0} | all-to-all | bytes 1048576 | tf_op jit(solution)/shard_map/all_to_all | solution.py:83
  134.0 0.5 broadcast.234
  134.5 1.9 reduce
  136.4 0.4 reshape.207
  136.8 1.0 convolution_convert_fusion.2
  137.9 0.8 copy.60
  138.7 0.0 all-gather.5.cloned.1.call-update
  138.7 0.0 reduce-scatter.2.cloned.1.call-start
  138.7 4.4 %fusion.45 = f32[1024,1024]{1,0:T(8,128)} fusion(bf16[1024,512]{1,0:T(8,128)(2,1)S(1)} %copy-done, bf16[512,1024]{1,0:T(8,128)(2,1)} %param.8), kind=kOutput, calls=%fused_computation.90 | convolution fusion | flops 1073741824 | bytes 6291456 | tf_op jit(solution)/shard_map/dot_general | solution.py:47
  143.2 0.0 reduce-scatter.2.cloned.1.call-update
  143.2 1.0 constant_dynamic-slice_fusion
  144.2 0.6 gather_fusion.2
  144.9 0.1 broadcast_select_fusion.1
  145.0 1.1 reshape.202
  146.1 5.9 %all-to-all-start.1 = ((bf16[32,2,2048]{2,1,0:T(2,128)(2,1)}), bf16[32,2,2048]{2,1,0:T(2,128)(2,1)S(1)}, u32[]{:S(2)}, u32[]{:S(2)}) async-start(bf16[32,2,2048]{2,1,0:T(2,128)(2,1)} %reshape.202), calls=%async_computation.2 | async-start | bytes 524288 | tf_op jit(solution)/shard_map/all_to_all | solution.py:38
  152.0 6.8 %all-to-all-done.1 = bf16[32,2,2048]{2,1,0:T(2,128)(2,1)S(1)} async-done(((bf16[32,2,2048]{2,1,0:T(2,128)(2,1)}), bf16[32,2,2048]{2,1,0:T(2,128)(2,1)S(1)}, u32[]{:S(2)}, u32[]{:S(2)}) %all-to-all-start.1) | async-done | bytes 262176 | tf_op jit(solution)/shard_map/all_to_all | solution.py:38
  158.8 0.4 reshape.203
  159.2 0.6 gather_fusion.3
  159.8 0.1 broadcast_select_fusion.6
  159.8 0.6 gather_fusion.4
  160.5 0.1 broadcast_select_fusion.3
  160.6 0.2 reshape.204
  160.8 22.2 %all_to_all.26 = bf16[16,2,2048]{2,1,0:T(2,128)(2,1)S(1)} all-to-all(bf16[16,2,2048]{2,1,0:T(2,128)(2,1)S(1)} %reshape.204), channel_id=1, replica_groups=mesh['dp'=32,'mp'=16] {'mp'}, dimensions={0} | all-to-all | bytes 262144 | tf_op jit(solution)/shard_map/all_to_all | solution.py:44
  183.0 0.2 reshape.205
  183.2 0.2 copy.48
  183.4 0.2 reshape.156
  183.6 0.2 fusion.8
  183.8 0.1 copy.49
  183.9 30.4 %all_gather.10 = bf16[1024,64]{1,0:T(8,128)(2,1)S(1)} all-gather(bf16[64,64]{1,0:T(8,128)(2,1)S(1)} %copy.49), channel_id=1, replica_groups=mesh['dp'=32,'mp'=16] {'mp'}, dimensions={0}, use_global_device_ids=true | all-gather | bytes 139264 | tf_op jit(solution)/shard_map/all_gather | solution.py:59
  214.2 0.3 fusion.6
  214.6 0.8 convolution_convert_fusion
  215.4 2.5 copy.54
  217.9 6.3 %all-to-all-start.3 = ((bf16[32,512,64]{1,2,0:T(8,128)(2,1)}), bf16[32,512,64]{1,2,0:T(8,128)(2,1)S(1)}, u32[]{:S(2)}, u32[]{:S(2)}) async-start(bf16[32,512,64]{1,2,0:T(8,128)(2,1)} %copy.54), calls=%async_computation.4 | async-start | bytes 4194304 | tf_op jit(solution)/shard_map/all_to_all | solution.py:82
  224.2 1.6 copy_bitcast_fusion
  225.8 2.8 fusion.15
  228.7 22.2 %all-to-all-done.3 = bf16[32,512,64]{1,2,0:T(8,128)(2,1)S(1)} async-done(((bf16[32,512,64]{1,2,0:T(8,128)(2,1)}), bf16[32,512,64]{1,2,0:T(8,128)(2,1)S(1)}, u32[]{:S(2)}, u32[]{:S(2)}) %all-to-all-start.3) | async-done | bytes 2097184 | tf_op jit(solution)/shard_map/all_to_all | solution.py:82
  250.9 1.2 fusion.3
  252.1 1.0 copy.61
  253.1 3.9 %fusion = bf16[1024,512]{1,0:T(8,128)(2,1)} fusion(f32[8,128,512]{2,1,0:T(8,128)S(1)} %copy-done.2, bf16[1024,1024]{1,0:T(8,128)(2,1)} %all-gather.3.cloned.1.call-done, bf16[512,1024]{1,0:T(8,128)(2,1)S(1)} %copy-done.5), kind=kOutput, calls=%fused_computation.6 | convolution fusion | flops 1074790400 | bytes 6291456 | tf_op jit(solution)/shard_map/nc,dc->nd/dot_general | solution.py:61
  256.9 3.3 %copy.62 = bf16[8,64,1024]{2,1,0:T(8,128)(2,1)} copy(bf16[8,64,1024]{1,0,2:T(8,128)(2,1)} %all-gather.5.cloned.1.call-done) | data formatting | bytes 2097152
  260.2 29.0 %reduce-scatter.2.cloned.1.call-done = f32[64,1024]{1,0:T(8,128)} async-done(((f32[1024,1024]{1,0:T(8,128)}), f32[64,1024]{1,0:T(8,128)}) %reduce-scatter.2.cloned.1.call-update) | async-done | bytes 262160 | tf_op jit(solution)/shard_map/reduce_scatter | solution.py:48
  289.3 1.9 fusion.7
  (19 shorter events, 0.1 us)
Async XLA Ops:
  7.2 44.4 %copy-start = (bf16[1024,512]{1,0:T(8,128)(2,1)S(1)}, bf16[1024,512]{1,0:T(8,128)(2,1)}, u32[]{:S(2)}) copy-start(bf16[1024,512]{1,0:T(8,128)(2,1)} %param.7) | copy-start | bytes 3145732
  7.2 107.3 %all-gather.3.cloned.1.call-start = ((), (), s32[]{:S(2)}) async-start(), calls=%async_computation.7 | async-start | bytes 2228224 | tf_op jit(solution)/shard_map/all_gather | solution.py:60
  12.5 36.9 %all-to-all-start = ((bf16[32,512,64]{1,2,0:T(8,128)(2,1)}), bf16[32,512,64]{1,2,0:T(8,128)(2,1)}, u32[]{:S(2)}, u32[]{:S(2)}) async-start(bf16[32,512,64]{1,2,0:T(8,128)(2,1)} %broadcast_select_fusion), calls=%async_computation.1 | async-start | bytes 4194304 | tf_op jit(solution)/shard_map/all_to_all | solution.py:37
  22.7 234.2 %all-gather.5.cloned.1.call-start = ((), (), s32[]{:S(2)}) async-start(), calls=%async_computation.8 | async-start | bytes 2228224 | tf_op jit(solution)/shard_map/all_gather | solution.py:91
  51.5 64.9 %copy-start.1 = (bf16[8,512,64]{1,2,0:T(8,128)(2,1)}, bf16[8,512,64]{1,2,0:T(8,128)(2,1)S(1)}, u32[]{:S(2)}) copy-start(bf16[8,512,64]{1,2,0:T(8,128)(2,1)S(1)} %gather_fusion.1) | copy-start | bytes 1572868
  114.4 1.3 copy-start.3
  138.7 150.6 %reduce-scatter.2.cloned.1.call-start = ((), (), s32[]{:S(2)}) async-start(), calls=%async_computation.6 | async-start | bytes 4456448 | tf_op jit(solution)/shard_map/reduce_scatter | solution.py:48
  146.1 12.7 %all-to-all-start.1 = ((bf16[32,2,2048]{2,1,0:T(2,128)(2,1)}), bf16[32,2,2048]{2,1,0:T(2,128)(2,1)S(1)}, u32[]{:S(2)}, u32[]{:S(2)}) async-start(bf16[32,2,2048]{2,1,0:T(2,128)(2,1)} %reshape.202), calls=%async_computation.2 | async-start | bytes 524288 | tf_op jit(solution)/shard_map/all_to_all | solution.py:38
  152.0 31.6 %copy-start.4 = (bf16[64,1024]{1,0:T(8,128)(2,1)S(1)}, bf16[64,1024]{1,0:T(8,128)(2,1)}, u32[]{:S(2)}) copy-start(bf16[64,1024]{1,0:T(8,128)(2,1)} %param.11) | copy-start | bytes 393220
  217.9 32.9 %all-to-all-start.3 = ((bf16[32,512,64]{1,2,0:T(8,128)(2,1)}), bf16[32,512,64]{1,2,0:T(8,128)(2,1)S(1)}, u32[]{:S(2)}, u32[]{:S(2)}) async-start(bf16[32,512,64]{1,2,0:T(8,128)(2,1)} %copy.54), calls=%async_computation.4 | async-start | bytes 4194304 | tf_op jit(solution)/shard_map/all_to_all | solution.py:82
  250.9 2.2 copy-start.2
  250.9 2.2 copy-start.5
Sparse Core Ops, SparseCore 0:
  10.1 77.7 all-gather.2
  138.8 70.7 all-gather.4
  212.5 76.7 reduce-scatter.1
where the time goes:
time: 298 us
  blocking collectives  131 us (44%)
  waiting for transfers between devices  85.3 us (29%)
  starting transfers between devices  22.5 us (8%)
  local copies, waits for them, and re-layouts  20.6 us (7%)
  matrix products  19.1 us (6%)
  between operations  14.1 us (5%)
  other arithmetic  4.96 us (2%)
    psum x1, blocking collectives, per_device(): down = lax.psum(down_part, 'mp').astype(jnp.bfloat16)  62.3 us
    all_gather x1, blocking collectives, per_device(): lax.all_gather(my_back, 'mp', axis=0, tiled=True)  30.4 us
    reduce_scatter x1, waiting for transfers between devices, per_device(): lax.psum_scatter(partial_value, 'mp', scatter_dimension=0, tiled=True)  29 us
    all_to_all x1, waiting for transfers between devices, per_device(): lax.all_to_all(send_a, 'dp', split_axis=0, concat_axis=0, tiled=True)  26.6 us
    all_to_all x1, waiting for transfers between devices, per_device(): lax.all_to_all(send_ga, 'dp', split_axis=0, concat_axis=0, tiled=True)  22.2 us
    all_to_all x1, blocking collectives, per_device(): lax.all_to_all(to_parts, 'mp', split_axis=0, concat_axis=0, tiled=True)  22.2 us
    all_to_all x1, blocking collectives, per_device(): lax.all_to_all(send_gb, 'dp', split_axis=0, concat_axis=0, tiled=True)  16.3 us
    all_to_all x1, starting transfers between devices, per_device(): lax.all_to_all(send_a, 'dp', split_axis=0, concat_axis=0, tiled=True)  10.2 us
  transfers between devices with their start and end apart: 6, of which 4 were waited for; matrix products, arithmetic and copies ran while one was open for 12% of the time, Pallas kernels for 0%

commit v1 on v0

--- a/solution.py
+++ b/solution.py
@@ -49,7 +49,7 @@
     down_part = jnp.einsum(
         "bnd,bdk->bnk", token_blocks, panel_a, preferred_element_type=jnp.float32
     )
-    down = lax.psum(down_part, "mp").astype(jnp.bfloat16)
+    down = jnp.sum(lax.all_gather(down_part, "mp"), axis=0).astype(jnp.bfloat16)
     my_down = lax.dynamic_slice_in_dim(down.reshape(rows, RANK), first_row, own_rows, 0)
     lifted = jnp.dot(my_down, my_up, preferred_element_type=jnp.float32)
     projected = (base + lifted).astype(jnp.bfloat16)

time: 298 us -> 373 us (1.25)
  the two profiles are of different devices: /device:TPU:4 before, /device:TPU:2 now
where the time goes in v1:
time: 373 us; the launch traced here: 372 us
  waiting for transfers between devices  215 us (58%)
  blocking collectives  59.6 us (16%)
  starting transfers between devices  29.1 us (8%)
  local copies, waits for them, and re-layouts  23.6 us (6%)
  matrix products  20.4 us (5%)
  between operations  14.1 us (4%)
  other arithmetic  9.46 us (3%)
    all_gather x1, waiting for transfers between devices, per_device(): grad_up = lax.all_gather(grad_share, 'mp', axis=2, tiled=True)  71.6 us
    all_gather x1, waiting for transfers between devices, per_device(): cot_all = lax.all_gather(cotangent, 'mp', axis=0, tiled=True)  68.8 us
    all_gather x1, blocking collectives, per_device(): lax.all_gather(my_back, 'mp', axis=0, tiled=True)  31.7 us
    all_to_all x1, blocking collectives, per_device(): lax.all_to_all(to_parts, 'mp', split_axis=0, concat_axis=0, tiled=True)  27.9 us
    all_to_all x1, waiting for transfers between devices, per_device(): lax.all_to_all(send_a, 'dp', split_axis=0, concat_axis=0, tiled=True)  27.9 us
    reduce_scatter x1, waiting for transfers between devices, per_device(): lax.psum_scatter(partial_value, 'mp', scatter_dimension=0, tiled=True)  17.5 us
    all_to_all x1, waiting for transfers between devices, per_device(): lax.all_to_all(send_ga, 'dp', split_axis=0, concat_axis=0, tiled=True)  13.5 us
    unnamed x26, local copies, waits for them, and re-layouts  10.9 us
  transfers between devices with their start and end apart: 8, of which 8 were waited for; matrix products, arithmetic and copies ran while one was open for 11% of the time, Pallas kernels for 0%

profile of v1, /device:TPU:2, one launch (start us, length us, event | category | flops | bytes accessed | tf_op | source)
XLA Modules:
  0.0 371.6 jit_solution(4139565892914986625)
XLA Ops:
  7.2 1.0 select_reduce_fusion
  8.1 0.1 reduce_sum.32
  8.2 0.1 fusion.43
  8.4 0.1 fusion.18
  8.5 1.7 gather_fusion
  10.3 1.6 broadcast_select_fusion
  11.8 10.3 %all-to-all-start = ((bf16[32,512,64]{1,2,0:T(8,128)(2,1)}), bf16[32,512,64]{1,2,0:T(8,128)(2,1)}, u32[]{:S(2)}, u32[]{:S(2)}) async-start(bf16[32,512,64]{1,2,0:T(8,128)(2,1)} %broadcast_select_fusion), calls=%async_computation.1 | async-start | bytes 4194304 | tf_op jit(solution)/shard_map/all_to_all | solution.py:37
  22.1 0.0 all-gather.9.cloned.1.call-start
  22.2 27.9 %all-to-all-done = bf16[32,512,64]{1,2,0:T(8,128)(2,1)} async-done(((bf16[32,512,64]{1,2,0:T(8,128)(2,1)}), bf16[32,512,64]{1,2,0:T(8,128)(2,1)}, u32[]{:S(2)}, u32[]{:S(2)}) %all-to-all-start) | async-done | bytes 2097184 | tf_op jit(solution)/shard_map/all_to_all | solution.py:37
  50.1 2.2 gather_fusion.1
  52.3 1.2 convolution_bitcast_fusion
  53.6 0.0 all-gather.5.cloned.1.call-start
  53.6 0.7 all-gather.5.cloned.1.call-update
  54.3 0.0 reduce-scatter.2.cloned.1.call-start
  54.4 3.2 fusion.45
  57.6 0.0 reduce-scatter.2.cloned.1.call-update
  57.6 1.0 constant_dynamic-slice_fusion
  58.6 0.6 gather_fusion.2
  59.3 0.1 broadcast_select_fusion.1
  59.4 1.1 reshape.202
  60.5 5.9 %all-to-all-start.1 = ((bf16[32,2,2048]{2,1,0:T(2,128)(2,1)}), bf16[32,2,2048]{2,1,0:T(2,128)(2,1)S(1)}, u32[]{:S(2)}, u32[]{:S(2)}) async-start(bf16[32,2,2048]{2,1,0:T(2,128)(2,1)} %reshape.202), calls=%async_computation.2 | async-start | bytes 524288 | tf_op jit(solution)/shard_map/all_to_all | solution.py:38
  66.5 7.7 %all-to-all-done.1 = bf16[32,2,2048]{2,1,0:T(2,128)(2,1)S(1)} async-done(((bf16[32,2,2048]{2,1,0:T(2,128)(2,1)}), bf16[32,2,2048]{2,1,0:T(2,128)(2,1)S(1)}, u32[]{:S(2)}, u32[]{:S(2)}) %all-to-all-start.1) | async-done | bytes 262176 | tf_op jit(solution)/shard_map/all_to_all | solution.py:38
  74.2 0.4 reshape.203
  74.6 0.6 gather_fusion.3
  75.1 0.1 broadcast_select_fusion.6
  75.2 0.6 gather_fusion.4
  75.8 0.1 broadcast_select_fusion.3
  75.9 0.2 reshape.204
  76.2 27.9 %all_to_all.25 = bf16[16,2,2048]{2,1,0:T(2,128)(2,1)S(1)} all-to-all(bf16[16,2,2048]{2,1,0:T(2,128)(2,1)S(1)} %reshape.204), channel_id=1, replica_groups=mesh['dp'=32,'mp'=16] {'mp'}, dimensions={0} | all-to-all | bytes 262144 | tf_op jit(solution)/shard_map/all_to_all | solution.py:44
  104.1 0.2 reshape.205
  104.3 0.2 copy.46
  104.5 0.2 reshape.155
  104.7 0.2 fusion.8
  104.9 0.1 copy.47
  105.0 31.7 %all_gather.18 = bf16[1024,64]{1,0:T(8,128)(2,1)S(1)} all-gather(bf16[64,64]{1,0:T(8,128)(2,1)S(1)} %copy.47), channel_id=1, replica_groups=mesh['dp'=32,'mp'=16] {'mp'}, dimensions={0}, use_global_device_ids=true | all-gather | bytes 139264 | tf_op jit(solution)/shard_map/all_gather | solution.py:59
  136.6 0.8 all-gather.9.cloned.1.call-done
  137.4 2.5 reduce_sum.35
  140.0 68.8 %all-gather.5.cloned.1.call-done = bf16[1024,1024]{1,0:T(8,128)(2,1)} async-done(((bf16[64,1024]{1,0:T(8,128)(2,1)}), bf16[1024,1024]{1,0:T(8,128)(2,1)}) %all-gather.5.cloned.1.call-update) | async-done | bytes 2097168 | tf_op jit(solution)/shard_map/all_gather | solution.py:60
  208.8 1.2 fusion.13
  210.0 0.7 fusion.11
  210.7 0.6 copy.56
  211.3 1.4 reshape.206
  212.8 7.4 %all-to-all-start.4 = ((f32[32,1,4096]{2,1,0:T(1,128)}), f32[32,1,4096]{2,1,0:T(1,128)S(1)}, u32[]{:S(2)}, u32[]{:S(2)}) async-start(f32[32,1,4096]{2,1,0:T(1,128)} %reshape.206), calls=%async_computation.5 | async-start | bytes 1048576 | tf_op jit(solution)/shard_map/all_to_all | solution.py:83
  220.2 0.3 fusion.6
  220.5 0.8 convolution_convert_fusion
  221.4 2.5 copy.52
  223.9 6.8 %all-to-all-done.4 = f32[32,1,4096]{2,1,0:T(1,128)S(1)} async-done(((f32[32,1,4096]{2,1,0:T(1,128)}), f32[32,1,4096]{2,1,0:T(1,128)S(1)}, u32[]{:S(2)}, u32[]{:S(2)}) %all-to-all-start.4) | async-done | bytes 524320 | tf_op jit(solution)/shard_map/all_to_all | solution.py:83
  230.7 0.8 copy-done.3
  231.5 5.2 %all-to-all-start.3 = ((bf16[32,512,64]{1,2,0:T(8,128)(2,1)}), bf16[32,512,64]{1,2,0:T(8,128)(2,1)S(1)}, u32[]{:S(2)}, u32[]{:S(2)}) async-start(bf16[32,512,64]{1,2,0:T(8,128)(2,1)} %copy.52), calls=%async_computation.4 | async-start | bytes 4194304 | tf_op jit(solution)/shard_map/all_to_all | solution.py:82
  236.7 0.2 all-gather.7.cloned.1.call-start
  236.9 0.6 broadcast.234
  237.5 3.8 %reduce = f32[32,4096]{1,0:T(8,128)} reduce(f32[32,1,4096]{2,1,0:T(1,128)} %copy-done.3, f32[]{:T(128)} %broadcast.234), dimensions={1}, to_apply=%all_to_all.19.reduce_sub_computation | reduce | bytes 1048580 | tf_op jit(solution)/shard_map/all_to_all | solution.py:83
  241.2 2.4 reshape.207
  243.7 2.9 convolution_convert_fusion.2
  246.5 1.7 copy.58
  248.3 2.9 fusion.15
  251.2 13.5 %all-to-all-done.3 = bf16[32,512,64]{1,2,0:T(8,128)(2,1)S(1)} async-done(((bf16[32,512,64]{1,2,0:T(8,128)(2,1)}), bf16[32,512,64]{1,2,0:T(8,128)(2,1)S(1)}, u32[]{:S(2)}, u32[]{:S(2)}) %all-to-all-start.3) | async-done | bytes 2097184 | tf_op jit(solution)/shard_map/all_to_all | solution.py:82
  264.6 1.2 fusion.3
  265.9 1.0 copy.59
  266.8 3.9 %fusion = bf16[1024,512]{1,0:T(8,128)(2,1)} fusion(f32[8,128,512]{2,1,0:T(8,128)S(1)} %copy-done.2, bf16[1024,1024]{1,0:T(8,128)(2,1)} %all-gather.5.cloned.1.call-done, bf16[512,1024]{1,0:T(8,128)(2,1)S(1)} %copy-done.8), kind=kOutput, calls=%fused_computation.6 | convolution fusion | flops 1074790400 | bytes 6291456 | tf_op jit(solution)/shard_map/nc,dc->nd/dot_general | solution.py:61
  270.7 17.5 %reduce-scatter.2.cloned.1.call-done = f32[64,1024]{1,0:T(8,128)} async-done(((f32[1024,1024]{1,0:T(8,128)}), f32[64,1024]{1,0:T(8,128)}) %reduce-scatter.2.cloned.1.call-update) | async-done | bytes 262160 | tf_op jit(solution)/shard_map/reduce_scatter | solution.py:48
  288.3 1.9 fusion.7
  290.2 71.6 %all-gather.7.cloned.1.call-done = bf16[8,64,1024]{1,0,2:T(8,128)(2,1)} async-done(((bf16[8,64,64]{1,0,2:T(8,128)(2,1)}), bf16[8,64,1024]{1,0,2:T(8,128)(2,1)}) %all-gather.7.cloned.1.call-update) | async-done | bytes 1048592 | tf_op jit(solution)/shard_map/all_gather | solution.py:91
  361.8 3.3 copy.60
  (29 shorter events, 0.2 us)
Async XLA Ops:
  7.2 45.1 %copy-start = (bf16[1024,512]{1,0:T(8,128)(2,1)S(1)}, bf16[1024,512]{1,0:T(8,128)(2,1)}, u32[]{:S(2)}) copy-start(bf16[1024,512]{1,0:T(8,128)(2,1)} %param.7) | copy-start | bytes 3145732
  11.8 38.3 %all-to-all-start = ((bf16[32,512,64]{1,2,0:T(8,128)(2,1)}), bf16[32,512,64]{1,2,0:T(8,128)(2,1)}, u32[]{:S(2)}, u32[]{:S(2)}) async-start(bf16[32,512,64]{1,2,0:T(8,128)(2,1)} %broadcast_select_fusion), calls=%async_computation.1 | async-start | bytes 4194304 | tf_op jit(solution)/shard_map/all_to_all | solution.py:37
  22.1 115.3 %all-gather.9.cloned.1.call-start = ((), (), s32[]{:S(2)}) async-start(), calls=%async_computation.9 | async-start | bytes 4456448 | tf_op jit(solution)/shard_map/all_gather | solution.py:52
  22.2 32.2 %copy-start.7 = (bf16[512,1024]{1,0:T(8,128)(2,1)S(1)}, bf16[512,1024]{1,0:T(8,128)(2,1)}, u32[]{:S(2)}) copy-start(bf16[512,1024]{1,0:T(8,128)(2,1)} %param.8) | copy-start | bytes 3145732
  52.3 5.3 %copy-start.1 = (bf16[8,512,64]{1,2,0:T(8,128)(2,1)}, bf16[8,512,64]{1,2,0:T(8,128)(2,1)S(1)}, u32[]{:S(2)}) copy-start(bf16[8,512,64]{1,2,0:T(8,128)(2,1)S(1)} %gather_fusion.1) | copy-start | bytes 1572868
  53.6 155.2 %all-gather.5.cloned.1.call-start = ((), (), s32[]{:S(2)}) async-start(), calls=%async_computation.7 | async-start | bytes 2228224 | tf_op jit(solution)/shard_map/all_gather | solution.py:60
  54.3 234.0 %reduce-scatter.2.cloned.1.call-start = ((), (), s32[]{:S(2)}) async-start(), calls=%async_computation.6 | async-start | bytes 4456448 | tf_op jit(solution)/shard_map/reduce_scatter | solution.py:48
  60.5 13.7 %all-to-all-start.1 = ((bf16[32,2,2048]{2,1,0:T(2,128)(2,1)}), bf16[32,2,2048]{2,1,0:T(2,128)(2,1)S(1)}, u32[]{:S(2)}, u32[]{:S(2)}) async-start(bf16[32,2,2048]{2,1,0:T(2,128)(2,1)} %reshape.202), calls=%async_computation.2 | async-start | bytes 524288 | tf_op jit(solution)/shard_map/all_to_all | solution.py:38
  66.5 38.2 %copy-start.6 = (bf16[64,1024]{1,0:T(8,128)(2,1)S(1)}, bf16[64,1024]{1,0:T(8,128)(2,1)}, u32[]{:S(2)}) copy-start(bf16[64,1024]{1,0:T(8,128)(2,1)} %param.11) | copy-start | bytes 393220
  140.0 70.1 %copy-start.4 = (bf16[8,128,64]{1,2,0:T(8,128)(2,1)}, bf16[8,128,64]{1,2,0:T(8,128)(2,1)S(1)}, u32[]{:S(2)}) copy-start(bf16[8,128,64]{1,2,0:T(8,128)(2,1)S(1)} %reduce_sum.35) | copy-start | bytes 393220
  212.8 17.9 %all-to-all-start.4 = ((f32[32,1,4096]{2,1,0:T(1,128)}), f32[32,1,4096]{2,1,0:T(1,128)S(1)}, u32[]{:S(2)}, u32[]{:S(2)}) async-start(f32[32,1,4096]{2,1,0:T(1,128)} %reshape.206), calls=%async_computation.5 | async-start | bytes 1048576 | tf_op jit(solution)/shard_map/all_to_all | solution.py:83
  230.7 0.8 copy-start.3
  231.5 33.1 %all-to-all-start.3 = ((bf16[32,512,64]{1,2,0:T(8,128)(2,1)}), bf16[32,512,64]{1,2,0:T(8,128)(2,1)S(1)}, u32[]{:S(2)}, u32[]{:S(2)}) async-start(bf16[32,512,64]{1,2,0:T(8,128)(2,1)} %copy.52), calls=%async_computation.4 | async-start | bytes 4194304 | tf_op jit(solution)/shard_map/all_to_all | solution.py:82
  236.7 125.1 %all-gather.7.cloned.1.call-start = ((), (), s32[]{:S(2)}) async-start(), calls=%async_computation.8 | async-start | bytes 2228224 | tf_op jit(solution)/shard_map/all_gather | solution.py:91
  264.6 2.2 copy-start.2
  264.6 2.2 copy-start.8
  266.8 3.9 %copy-start.5 = (bf16[8,128,64]{1,2,0:T(8,128)(2,1)S(1)}, bf16[8,128,64]{1,2,0:T(8,128)(2,1)}, u32[]{:S(2)}) copy-start(bf16[8,128,64]{1,2,0:T(8,128)(2,1)} %copy-done.4) | copy-start | bytes 393220
Sparse Core Ops, SparseCore 0:
  53.7 83.6 all-gather.8
  139.5 69.2 all-gather.4
  211.6 76.5 reduce-scatter.1
  290.8 70.9 all-gather.6
